TPU v7x, 256 devices: a whole 4x4x8 slice. The times are simulated.
256 devices in a mesh: dp: 16 (over y, x), seq: 16 (over z, core).
Axes of the slice: x: 4, y: 4, z: 8, core: 2. Of those that a mesh axis runs over, the one named last changes fastest.
Arguments:
- ssm_input: bfloat16 [16, 2048, 2048], P('dp', 'seq'), may hold values from -6 to 6
- gate_input: bfloat16 [16, 2048, 2048], P('dp', 'seq'), may hold values from -6 to 6
- grad_gated: bfloat16 [16, 2048, 2048], P('dp', 'seq'), may hold values from -6 to 6
- x_proj: bfloat16 [2048, 96], replicated, may hold values from -0.125 to 0.125
- dt_proj: bfloat16 [64, 2048], replicated, may hold values from -0.75 to 0.75
- dt_bias: float32 [2048], replicated, may hold values from -14 to -2
- fid_bias: float32 [2, 2048], replicated, may hold values from -3 to 3
- a_log: float32 [2048, 16], replicated, may hold values from 0 to 2.77
- skip_gain: float32 [2048], replicated, may hold values from 0.5 to 1.5
- rec_lengths: int32 [16], P('dp'), may hold values from 512 to 2048, as said below
- fid_labels: int32 [16], P('dp'), may hold values from 0 to 1
Outputs:
- gated: bfloat16 [16, 2048, 2048], P('dp', 'seq')
- grad_input: bfloat16 [16, 2048, 2048], P('dp', 'seq')
- grad_gate: bfloat16 [16, 2048, 2048], P('dp', 'seq')
- grad_x_proj: float32 [2048, 96], P('dp')
- grad_dt_proj: float32 [64, 2048], P(None, 'dp')
- grad_a_log: float32 [2048, 16], P('dp')
- grad_skip: float32 [2048], P('dp')
- grad_dt_bias: float32 [2048], P('dp')
- grad_fid_bias: float32 [2, 2048], P(None, 'dp')
Inputs may be any that keep to these rules, and one draw needn't show every extreme that they name: `rec_lengths`: each record's count of valid time steps; in every draw some record is 2048 long.
All inputs are finite; a program needn't handle non-finite values.
Results may differ from a plain program's by a relative error of at most 0.0068.
Values sent between devices are 32-bit elements; how exact they have to be, the bound alone decides.
A program may use at most 64 MiB of HBM per device.

v0:
```python
import jax
import jax.numpy as jnp
from jax import lax
from jax.sharding import PartitionSpec as P


def passed_along(block, axis, distance):
    devices = range(lax.axis_size(axis))
    route = [(i - distance, i) for i in devices if i - distance in devices]
    return lax.ppermute(block, axis, route)


def run_block(h_now, a_trans, pieces):
    step_blk, b_blk, c_blk, val_blk = pieces
    outputs = []
    for position in range(step_blk.shape[0]):
        decay = jnp.exp(a_trans * step_blk[position][None, :])
        h_now = (
            decay * h_now
            + b_blk[position][:, None] * (step_blk[position] * val_blk[position])[None, :]
        )
        outputs.append(jnp.sum(c_blk[position][:, None] * h_now, axis=0))
    return (h_now, jnp.stack(outputs))


def to_blocks(array, turns):
    return array.reshape((turns, array.shape[0] // turns) + array.shape[1:])


def forward_record(h_start, a_trans, pieces, turns):
    blocks = tuple((to_blocks(piece, turns) for piece in pieces))

    def advance(h_now, blk_pieces):
        h_next, outputs = run_block(h_now, a_trans, blk_pieces)
        return (h_next, (h_now, outputs))

    h_last, (checks, outputs) = lax.scan(advance, h_start, blocks)
    return (h_last, checks, outputs.reshape((-1, outputs.shape[-1])))


def pull_record(stepsize, c_proj, y_grad, a_trans, turns):
    blocks = (to_blocks(stepsize, turns), to_blocks(c_proj, turns), to_blocks(y_grad, turns))

    def pull_retreat(adjoint, blk_pieces):
        step_blk, c_blk, grad_blk = blk_pieces
        for position in range(step_blk.shape[0] - 1, -1, -1):
            gathered = c_blk[position][:, None] * grad_blk[position][None, :] + adjoint
            adjoint = jnp.exp(a_trans * step_blk[position][None, :]) * gathered
        return (adjoint, None)

    adjoint, _ = lax.scan(pull_retreat, jnp.zeros_like(a_trans), blocks, reverse=True)
    return adjoint


def backward_record(checks, end_grad, a_trans, pieces, y_grad, turns):
    blocks = tuple((to_blocks(piece, turns) for piece in pieces))
    grad_blocks = to_blocks(y_grad, turns)

    def backward_retreat(carry, inputs):
        adjoint, a_total = carry
        h_in, blk_pieces, grad_blk = inputs
        _, block_back = jax.vjp(run_block, h_in, a_trans, blk_pieces)
        h_grad, a_part, piece_grads = block_back((adjoint, grad_blk))
        return ((h_grad, a_total + a_part), piece_grads)

    (_, a_grad), piece_grads = lax.scan(
        backward_retreat,
        (end_grad, jnp.zeros_like(a_trans)),
        (checks, blocks, grad_blocks),
        reverse=True,
    )
    flat = tuple((grad.reshape((-1,) + grad.shape[2:]) for grad in piece_grads))
    return flat + (a_grad,)


def per_device(
    ssm_input,
    gate_input,
    grad_gated,
    x_proj,
    dt_proj,
    dt_bias,
    fid_bias,
    a_log,
    skip_gain,
    rec_lengths,
    fid_labels,
):
    records, seg_len, channels = ssm_input.shape
    low_rank = dt_proj.shape[0]
    states = a_log.shape[1]
    fidelities = fid_bias.shape[0]
    turns = min(16, seg_len)
    projected = jnp.einsum("rle,ek->rlk", ssm_input, x_proj, preferred_element_type=jnp.float32)
    low = projected[:, :, :low_rank].astype(jnp.bfloat16)
    b_proj = projected[:, :, low_rank : low_rank + states]
    c_proj = projected[:, :, low_rank + states :]
    onehot = (fid_labels[:, None] == jnp.arange(fidelities, dtype=jnp.int32)[None, :]).astype(
        jnp.float32
    )
    fid_shift = jnp.dot(onehot, fid_bias, precision=lax.Precision.HIGHEST)
    dt_raw = (
        jnp.einsum("rlk,ke->rle", low, dt_proj, preferred_element_type=jnp.float32)
        + dt_bias
        + fid_shift[:, None, :]
    )
    positions = lax.axis_index("seq") * seg_len + jnp.arange(seg_len, dtype=jnp.int32)
    live = (positions[None, :] < rec_lengths[:, None]).astype(jnp.float32)[:, :, None]
    stepsize = jax.nn.softplus(dt_raw) * live
    a_matrix = -jnp.exp(a_log)
    a_trans = a_matrix.T
    values = ssm_input.astype(jnp.float32)
    s_total = jnp.sum(stepsize, axis=1)

    def zero_ends(pieces):
        h_last, _, _ = forward_record(jnp.zeros_like(a_trans), a_trans, pieces, turns)
        return h_last

    h_end = lax.map(zero_ends, (stepsize, b_proj, c_proj, values))
    gate_value = gate_input.astype(jnp.float32)
    gate_sigmoid = jax.nn.sigmoid(gate_value)
    gate_silu = gate_value * gate_sigmoid
    out_grad = grad_gated.astype(jnp.float32) * live
    y_grad = out_grad * gate_silu

    def pulls(pieces):
        step_rec, c_rec, grad_rec = pieces
        return pull_record(step_rec, c_rec, grad_rec, a_trans, turns)

    h_pull = lax.map(pulls, (stepsize, c_proj, y_grad))
    decay_total = jnp.exp(a_trans[None] * s_total[:, None, :])

    def forward_turn(turn, incoming):
        return passed_along(decay_total * incoming + h_end, "seq", 1)

    def backward_turn(turn, incoming):
        return passed_along(h_pull + decay_total * incoming, "seq", -1)

    h_start = lax.fori_loop(0, lax.axis_size("seq") - 1, forward_turn, jnp.zeros_like(h_end))
    end_grad = lax.fori_loop(0, lax.axis_size("seq") - 1, backward_turn, jnp.zeros_like(h_pull))

    def full_forward(pieces):
        start_rec, step_rec, b_rec, c_rec, val_rec = pieces
        _, checks, outputs = forward_record(
            start_rec, a_trans, (step_rec, b_rec, c_rec, val_rec), turns
        )
        return (checks, outputs)

    checks, y_ssm = lax.map(full_forward, (h_start, stepsize, b_proj, c_proj, values))
    y_full = y_ssm + skip_gain * values
    gated = (y_full * gate_silu * live).astype(jnp.bfloat16)
    grad_gate = (
        out_grad * y_full * (gate_sigmoid * (1.0 + gate_value * (1.0 - gate_sigmoid)))
    ).astype(jnp.bfloat16)

    def full_backward(pieces):
        check_rec, end_rec, step_rec, b_rec, c_rec, val_rec, grad_rec = pieces
        return backward_record(
            check_rec, end_rec, a_trans, (step_rec, b_rec, c_rec, val_rec), grad_rec, turns
        )

    step_grad, b_grad, c_grad, u_grad, a_grads = lax.map(
        full_backward, (checks, end_grad, stepsize, b_proj, c_proj, values, y_grad)
    )
    a_grad = jnp.sum(a_grads, axis=0).T
    dt_grad = step_grad * live * jax.nn.sigmoid(dt_raw)
    dt_grad_b = dt_grad.astype(jnp.bfloat16)
    dt_proj_part = jnp.einsum("rlk,rle->ek", low, dt_grad_b, preferred_element_type=jnp.float32)
    low_grad = jnp.einsum("rle,ke->rlk", dt_grad_b, dt_proj, preferred_element_type=jnp.float32)
    proj_grad = jnp.concatenate([low_grad, b_grad, c_grad], axis=2).astype(jnp.bfloat16)
    x_proj_part = jnp.einsum(
        "rle,rlk->ek", ssm_input, proj_grad, preferred_element_type=jnp.float32
    )
    input_grad = (
        u_grad
        + y_grad * skip_gain
        + jnp.einsum("rlk,ek->rle", proj_grad, x_proj, preferred_element_type=jnp.float32)
    )
    grad_input = input_grad.astype(jnp.bfloat16)
    dt_sums = jnp.sum(dt_grad, axis=1)
    packed = jnp.concatenate(
        [
            x_proj_part,
            dt_proj_part,
            a_grad * a_matrix,
            jnp.sum(y_grad * values, axis=(0, 1))[:, None],
            jnp.sum(dt_sums, axis=0)[:, None],
            jnp.dot(dt_sums.T, onehot, precision=lax.Precision.HIGHEST),
        ],
        axis=1,
    )
    totals = lax.psum(packed, "seq")
    shares = lax.psum_scatter(totals, "dp", scatter_dimension=0, tiled=True)
    col_x = low_rank + 2 * states
    col_dt = col_x + low_rank
    col_a = col_dt + states
    grad_x_proj = shares[:, :col_x]
    grad_dt_proj = shares[:, col_x:col_dt].T
    grad_a_log = shares[:, col_dt:col_a]
    grad_skip = shares[:, col_a]
    grad_dt_bias = shares[:, col_a + 1]
    grad_fid_bias = shares[:, col_a + 2 :].T
    return (
        gated,
        grad_input,
        grad_gate,
        grad_x_proj,
        grad_dt_proj,
        grad_a_log,
        grad_skip,
        grad_dt_bias,
        grad_fid_bias,
    )


def solution(mesh):
    in_specs = (
        P("dp", "seq", None),
        P("dp", "seq", None),
        P("dp", "seq", None),
        P(),
        P(),
        P(),
        P(),
        P(),
        P(),
        P("dp"),
        P("dp"),
    )
    out_specs = (
        P("dp", "seq", None),
        P("dp", "seq", None),
        P("dp", "seq", None),
        P("dp", None),
        P(None, "dp"),
        P("dp", None),
        P("dp"),
        P("dp"),
        P(None, "dp"),
    )
    return jax.shard_map(
        per_device, mesh=mesh, in_specs=in_specs, out_specs=out_specs, check_vma=False
    )
```

profile of v0, /device:TPU:1, one launch (start us, length us, event | category | flops | bytes accessed | tf_op | source)
XLA Modules:
  0.0 812.1 jit_solution(1618265109441323945)
XLA Ops:
  14.2 38.7 %while.126 = (s32[]{:T(128)}, f32[16,2048]{1,0:T(8,128)S(1)}, f32[16,8,2048]{2,1,0:T(8,128)}, f32[16,2048]{1,0:T(8,128)S(1)}, f32[16,8,16]{2,1,0:T(8,128)}, /*in...) while((s32[]{:T(128)}, f32[16,2048]{1,0:T(8,128)S(1)}, ...), condition=%wide.region_2.3_spmd.clone, body=%wide.region_1.2_spmd.clone.sunk | while | flops 1097738 | bytes 985871 | solution.py:37
  54.0 95.3 %while.123 = (s32[]{:T(128)}, f32[1,16,2048]{2,1,0:T(8,128)S(1)}, f32[1,16,2048]{2,1,0:T(8,128)S(1)}, f32[1,16,2048]{2,1,0:T(8,128)S(1)}, s32[]{:T(128)}) while((s32[]{:T(128)}, f32[1,16,2048]{2,1,0:T(8,128)S(1)}, f32[1,16,2048]{2,1,0:T(8,128)S(1)}, f32[1,16,2048]{2,1,0:T(8,128)S(1)}, s32[]{:T(128)}) %tuple.429), condition=%wide.region_4.5_spmd, body=%wide.region_3.4_spmd.sunk | while | flops 65538 | bytes 1048677 | solution.py:139
  54.0 4.9 collective-permute-start
  59.0 1.9 collective-permute-done
  60.9 4.4 collective-permute-start
  65.3 1.9 collective-permute-done
  67.2 4.4 collective-permute-start
  71.6 1.9 collective-permute-done
  73.5 4.4 collective-permute-start
  79.8 4.4 collective-permute-start
  86.2 4.4 collective-permute-start
  92.5 4.4 collective-permute-start
  96.8 1.9 collective-permute-done
  98.8 4.4 collective-permute-start
  105.1 4.4 collective-permute-start
  111.4 4.4 collective-permute-start
  117.7 4.4 collective-permute-start
  124.0 4.4 collective-permute-start
  128.4 1.9 collective-permute-done
  130.3 4.4 collective-permute-start
  136.7 4.4 collective-permute-start
  141.0 1.9 collective-permute-done
  143.0 4.4 collective-permute-start
  150.3 73.6 %while.124 = (s32[]{:T(128)}, f32[16,2048]{1,0:T(8,128)S(1)}, f32[16,16,2048]{2,1,0:T(8,128)}, f32[16,8,2048]{2,1,0:T(8,128)}, f32[16,8,2048]{2,1,0:T(8,128)}, /...) while((s32[]{:T(128)}, f32[16,2048]{1,0:T(8,128)S(1)}, ...), condition=%wide.region_14.15_spmd, body=%wide.region_5.0_spmd.sunk | while | flops 2359305 | bytes 2333341 | solution.py:37
  224.0 4.0 fusion.44
  228.0 70.4 %while.127 = (s32[]{:T(128)}, f32[16,2048]{1,0:T(8,128)S(1)}, f32[16,8,2048]{2,1,0:T(8,128)}, f32[16,2048]{1,0:T(8,128)S(1)}, f32[16,8,16]{2,1,0:T(8,128)}, /*in...) while((s32[]{:T(128)}, f32[16,2048]{1,0:T(8,128)S(1)}, ...), condition=%wide.region_16.17_spmd.clone, body=%wide.region_15.16_spmd.clone.sunk | while | flops 1081355 | bytes 789283 | solution.py:51
  228.0 1.9 constant_dynamic-slice_fusion.91
  232.4 2.0 constant_dynamic-slice_fusion.91
  236.8 2.0 constant_dynamic-slice_fusion.91
  241.1 2.0 constant_dynamic-slice_fusion.91
  245.5 2.0 constant_dynamic-slice_fusion.91
  249.9 2.0 constant_dynamic-slice_fusion.91
  254.3 2.0 constant_dynamic-slice_fusion.91
  258.7 2.0 constant_dynamic-slice_fusion.91
  263.1 2.0 constant_dynamic-slice_fusion.91
  267.5 2.0 constant_dynamic-slice_fusion.91
  271.8 2.0 constant_dynamic-slice_fusion.91
  276.2 2.0 constant_dynamic-slice_fusion.91
  280.6 2.0 constant_dynamic-slice_fusion.91
  285.0 2.0 constant_dynamic-slice_fusion.91
  289.4 2.2 constant_dynamic-slice_fusion.91
  294.0 2.0 constant_dynamic-slice_fusion.91
  299.4 114.7 %while.125 = (s32[]{:T(128)}, f32[1,16,2048]{2,1,0:T(8,128)S(1)}, f32[1,16,2048]{2,1,0:T(8,128)S(1)}, f32[1,16,2048]{2,1,0:T(8,128)S(1)}, s32[]{:T(128)}) while((s32[]{:T(128)}, f32[1,16,2048]{2,1,0:T(8,128)S(1)}, f32[1,16,2048]{2,1,0:T(8,128)S(1)}, f32[1,16,2048]{2,1,0:T(8,128)S(1)}, s32[]{:T(128)}) %tuple.428), condition=%wide.region_18.19_spmd, body=%wide.region_17.18_spmd.sunk | while | flops 65538 | bytes 1048677 | solution.py:140
  301.4 5.7 collective-permute-done.1
  309.1 5.4 collective-permute-done.1
  316.5 6.3 collective-permute-done.1
  324.7 5.4 collective-permute-done.1
  332.1 6.3 collective-permute-done.1
  340.3 5.4 collective-permute-done.1
  347.7 6.3 collective-permute-done.1
  355.9 5.6 collective-permute-done.1
  363.5 5.6 collective-permute-done.1
  371.0 5.6 collective-permute-done.1
  378.5 5.6 collective-permute-done.1
  386.0 5.6 collective-permute-done.1
  393.6 5.6 collective-permute-done.1
  401.1 5.6 collective-permute-done.1
  408.6 5.6 collective-permute-done.1
  416.4 175.0 %while.128 = (s32[]{:T(128)}, f32[16,2048]{1,0:T(8,128)S(1)}, f32[16,2048]{1,0:T(8,128)S(1)}, f32[16,8,2048]{2,1,0:T(8,128)}, bf16[16,8,16]{2,1,0:T(8,128)(2,1)S...) while((s32[]{:T(128)}, f32[16,2048]{1,0:T(8,128)S(1)}, ...), condition=%wide.region_52.53_spmd.clone, body=%wide.region_19.52_spmd.clone.sunk | while | flops 8701451 | bytes 6086559 | solution.py:66
  482.3 1.9 constant_dynamic-slice_fusion.93
  594.4 3.7 concatenate.18
  598.1 93.7 %reduce-scatter.2.cloned.1.call-done = f32[128,180]{0,1:T(8,128)} async-done(((f32[2048,180]{0,1:T(8,128)}), f32[128,180]{0,1:T(8,128)}) %reduce-scatter.2.cloned.1.call-update) | async-done | bytes 92176 | tf_op jit(solution)/shard_map/reduce_scatter | solution.py:193
  691.9 2.4 fusion.35
  694.3 104.4 %all-reduce.42.cloned.1.call-done = f32[128,180]{0,1:T(8,128)} async-done(((f32[128,180]{0,1:T(8,128)}), f32[128,180]{0,1:T(8,128)}) %all-reduce.42.cloned.1.call-update) | async-done | bytes 92176 | tf_op jit(solution)/shard_map/psum | solution.py:192
  (1177 shorter events, 385.7 us)
Async XLA Ops:
  7.2 1.4 copy-start
  7.2 4.8 copy-start.4
  7.2 4.8 copy-start.21
  7.2 5.0 copy-start.7
  7.2 5.0 copy-start.15
  7.2 684.6 %reduce-scatter.2.cloned.1.call-start = ((), (), s32[]{:S(2)}) async-start(), calls=%async_computation.1 | async-start | bytes 1601536 | tf_op jit(solution)/shard_map/reduce_scatter | solution.py:193
  9.9 4.3 copy-start.10
  12.2 211.7 %copy-start.18 = (f32[128]{0:T(128)}, f32[128]{0:T(128)S(1)}, u32[]{:S(2)}) copy-start(f32[128]{0:T(128)S(1)} %compare_convert_fusion) | copy-start | bytes 1540
  52.9 1.0 copy-start.2
  54.0 6.9 collective-permute-start
  60.9 6.3 collective-permute-start
  67.2 6.3 collective-permute-start
  73.5 6.3 collective-permute-start
  79.8 6.3 collective-permute-start
  86.2 6.3 collective-permute-start
  92.5 6.3 collective-permute-start
  98.8 6.3 collective-permute-start
  105.1 6.3 collective-permute-start
  111.4 6.3 collective-permute-start
  117.7 6.3 collective-permute-start
  124.0 6.3 collective-permute-start
  130.3 6.3 collective-permute-start
  136.7 6.3 collective-permute-start
  143.0 6.3 collective-permute-start
  150.3 73.6 %copy-start.1 = (bf16[1,128,2048]{2,1,0:T(8,128)(2,1)S(1)}, bf16[1,128,2048]{2,1,0:T(8,128)(2,1)}, u32[]{:S(2)}) copy-start(bf16[1,128,2048]{2,1,0:T(8,128)(2,1)} %param.23) | copy-start | bytes 1572868
  150.3 73.6 %copy-start.16 = (f32[2048]{0:T(1024)S(1)}, f32[2048]{0:T(1024)}, u32[]{:S(2)}) copy-start(f32[2048]{0:T(1024)} %param.31) | copy-start | bytes 24580
  298.4 1.0 copy-start.3
  299.5 7.6 collective-permute-start.1
  307.1 7.4 collective-permute-start.1
  314.5 8.2 %collective-permute-start.1 = (f32[1,16,2048]{2,1,0:T(8,128)S(1)}, f32[1,16,2048]{2,1,0:T(8,128)S(1)}, u32[]{:S(2)}, u32[]{:S(2)}) collective-permute-start(f32[1,16,2048]{2,1,0:T(8,128)S(1)} %multiply_add_fusion.34), channel_id=1, source_target_pairs={{1,0},{2,1},{3,2},{4,3},{5,4},{6,5},{7,6},{8,7},{9,8},{10,9},{11,1... | collective-permute-start | bytes 393224 | tf_op jit(solution)/shard_map/while/body/eval_jaxpr/ppermute | solution.py:10
  322.8 7.4 collective-permute-start.1
  330.1 8.2 %collective-permute-start.1 = (f32[1,16,2048]{2,1,0:T(8,128)S(1)}, f32[1,16,2048]{2,1,0:T(8,128)S(1)}, u32[]{:S(2)}, u32[]{:S(2)}) collective-permute-start(f32[1,16,2048]{2,1,0:T(8,128)S(1)} %multiply_add_fusion.34), channel_id=1, source_target_pairs={{1,0},{2,1},{3,2},{4,3},{5,4},{6,5},{7,6},{8,7},{9,8},{10,9},{11,1... | collective-permute-start | bytes 393224 | tf_op jit(solution)/shard_map/while/body/eval_jaxpr/ppermute | solution.py:10
  338.4 7.4 collective-permute-start.1
  345.8 8.2 %collective-permute-start.1 = (f32[1,16,2048]{2,1,0:T(8,128)S(1)}, f32[1,16,2048]{2,1,0:T(8,128)S(1)}, u32[]{:S(2)}, u32[]{:S(2)}) collective-permute-start(f32[1,16,2048]{2,1,0:T(8,128)S(1)} %multiply_add_fusion.34), channel_id=1, source_target_pairs={{1,0},{2,1},{3,2},{4,3},{5,4},{6,5},{7,6},{8,7},{9,8},{10,9},{11,1... | collective-permute-start | bytes 393224 | tf_op jit(solution)/shard_map/while/body/eval_jaxpr/ppermute | solution.py:10
  354.0 7.5 collective-permute-start.1
  361.5 7.5 collective-permute-start.1
  369.1 7.5 collective-permute-start.1
  376.6 7.5 collective-permute-start.1
  384.1 7.5 collective-permute-start.1
  391.6 7.5 collective-permute-start.1
  399.1 7.5 collective-permute-start.1
  406.7 7.5 collective-permute-start.1
  416.4 175.1 %copy-start.19 = (f32[128]{0:T(128)S(1)}, f32[128]{0:T(128)}, u32[]{:S(2)}) copy-start(f32[128]{0:T(128)} %copy-done.18) | copy-start | bytes 1540
  591.5 1.7 copy-start.8
  591.5 2.0 copy-start.11
  591.5 2.4 copy-start.5
  593.1 1.1 copy-start.14
  593.5 0.8 copy-start.12
  594.3 97.5 %copy-start.6 = (f32[16,8,2048]{2,1,0:T(8,128)S(1)}, f32[16,8,2048]{2,1,0:T(8,128)}, u32[]{:S(2)}) copy-start(f32[16,8,2048]{2,1,0:T(8,128)} %get-tuple-element.644) | copy-start | bytes 3145732
  594.3 97.5 %copy-start.9 = (bf16[1,128,2048]{2,1,0:T(8,128)(2,1)S(1)}, bf16[1,128,2048]{2,1,0:T(8,128)(2,1)}, u32[]{:S(2)}) copy-start(bf16[1,128,2048]{2,1,0:T(8,128)(2,1)} %param.24) | copy-start | bytes 1572868
  594.3 97.5 %copy-start.13 = (bf16[128,64]{0,1:T(8,128)(2,1)S(1)}, bf16[128,64]{0,1:T(8,128)(2,1)}, u32[]{:S(2)}) copy-start(bf16[128,64]{0,1:T(8,128)(2,1)} %copy-done.12) | copy-start | bytes 49156
  594.3 97.5 %copy-start.17 = (f32[2048]{0:T(1024)S(1)}, f32[2048]{0:T(1024)}, u32[]{:S(2)}) copy-start(f32[2048]{0:T(1024)} %param.31) | copy-start | bytes 24580
  594.3 97.5 %copy-start.20 = (f32[128]{0:T(128)S(1)}, f32[128]{0:T(128)}, u32[]{:S(2)}) copy-start(f32[128]{0:T(128)} %copy-done.18) | copy-start | bytes 1540
  598.0 200.6 %all-reduce.42.cloned.1.call-start = ((), (), s32[]{:S(2)}) async-start(), calls=%async_computation.2 | async-start | bytes 188416 | tf_op jit(solution)/shard_map/psum | solution.py:192
Sparse Core Ops, SparseCore 0:
  598.2 93.5 reduce-scatter.1
  694.1 104.5 all-reduce.41
where the time goes:
time: 823 us; the launch traced here: 812 us
  waiting for transfers between devices  312 us (38%)
  local copies, waits for them, and re-layouts  223 us (27%)
  other arithmetic  155 us (19%)
  starting transfers between devices  94.8 us (12%)
  between operations  15.8 us (2%)
    ppermute x30, waiting for transfers between devices, passed_along(): return lax.ppermute(block, axis, route)  114 us
    psum x1, waiting for transfers between devices, per_device(): totals = lax.psum(packed, 'seq')  104 us
    ppermute x30, starting transfers between devices, passed_along(): return lax.ppermute(block, axis, route)  94.7 us
    reduce_scatter x1, waiting for transfers between devices, per_device(): shares = lax.psum_scatter(totals, 'dp', scatter_dimension=0, tiled=True)  93.7 us
    slice x48, local copies, waits for them, and re-layouts, run_block(): val_blk[position]  69.5 us
    dynamic_slice x64, local copies, waits for them, and re-layouts, forward_record(): h_last, (checks, outputs) = lax.scan(advance, h_start, blocks)  44.5 us
    reduce_sum x80, other arithmetic, run_block(): outputs.append(jnp.sum(c_blk[position][:, None] * h_now, axis=0))  36.7 us
    reduce_sum x32, other arithmetic, run_block(): decay = jnp.exp(a_trans * step_blk[position][None, :])  33.4 us
  transfers between devices with their start and end apart: 32, of which 32 were waited for; matrix products, arithmetic and copies ran while one was open for 0% of the time, Pallas kernels for 0%

commit v1 on v0

--- a/solution.py
+++ b/solution.py
@@ -2,6 +2,20 @@
 import jax.numpy as jnp
 from jax import lax
 from jax.sharding import PartitionSpec as P
+from jax.lax import axis_size, ppermute
+
+
+def wait_the_tiles(q_in):
+    devs = axis_size("seq")
+    earlier, part_now = (q_in, 0)
+    while 1 << part_now < devs:
+        sheets = []
+        for kk in range(devs):
+            sheets.append((kk, kk ^ 1 << part_now))
+        left_arr = ppermute(earlier, "seq", perm=sheets)
+        earlier = earlier + left_arr
+        part_now = part_now + 1
+    return earlier
 
 
 def passed_along(block, axis, distance):
@@ -189,7 +203,7 @@
         ],
         axis=1,
     )
-    totals = lax.psum(packed, "seq")
+    totals = wait_the_tiles(packed)
     shares = lax.psum_scatter(totals, "dp", scatter_dimension=0, tiled=True)
     col_x = low_rank + 2 * states
     col_dt = col_x + low_rank

time: 823 us -> 864 us (1.050)
  waiting for transfers between devices: 312 us -> 356 us
  starting transfers between devices: 94.8 us -> 120 us
  local copies, waits for them, and re-layouts: 223 us -> 206 us
  other arithmetic: 155 us -> 143 us
    ppermute x0 -> x4, waiting for transfers between devices: none -> 169 us  [wait_the_tiles(): left_arr = ppermute(earlier, 'seq', perm=sheets)]
    psum x1 -> x0, waiting for transfers between devices: 104 us -> none  [per_device(): totals = lax.psum(packed, 'seq')]
    ppermute x0 -> x4, starting transfers between devices: none -> 25.1 us  [wait_the_tiles(): left_arr = ppermute(earlier, 'seq', perm=sheets)]
    reduce_scatter x1, waiting for transfers between devices: 93.7 us -> 72.5 us  [per_device(): shares = lax.psum_scatter(totals, 'dp', scatter_dimension=0, tiled=True)]
    mul x16, other arithmetic: 17.6 us -> 4.02 us  [pull_retreat(): adjoint = jnp.exp(a_trans * step_blk[position][None, :]) * gathered]
    mul x16, local copies, waits for them, and re-layouts: 9.97 us -> 0.13 us  [pull_retreat(): gathered = c_blk[position][:, None] * grad_blk[position][None, :] + adjoint]
  transfers between devices with their start and end apart: 32 -> 35, of which waited for: 32 -> 35; matrix products, arithmetic and copies ran while one was open for 0% -> 0% of each run, Pallas kernels for 0% -> 0%
where the time goes in v1:
time: 864 us; the launch traced here: 853 us
  waiting for transfers between devices  356 us (41%)
  local copies, waits for them, and re-layouts  206 us (24%)
  other arithmetic  143 us (17%)
  starting transfers between devices  120 us (14%)
  between operations  15.8 us (2%)
    ppermute x4, waiting for transfers between devices, wait_the_tiles(): left_arr = ppermute(earlier, 'seq', perm=sheets)  169 us
    ppermute x30, waiting for transfers between devices, passed_along(): return lax.ppermute(block, axis, route)  114 us
    ppermute x30, starting transfers between devices, passed_along(): return lax.ppermute(block, axis, route)  94.7 us
    reduce_scatter x1, waiting for transfers between devices, per_device(): shares = lax.psum_scatter(totals, 'dp', scatter_dimension=0, tiled=True)  72.5 us
    slice x48, local copies, waits for them, and re-layouts, run_block(): val_blk[position]  69.5 us
    dynamic_slice x64, local copies, waits for them, and re-layouts, forward_record(): h_last, (checks, outputs) = lax.scan(advance, h_start, blocks)  44.5 us
    reduce_sum x80, other arithmetic, run_block(): outputs.append(jnp.sum(c_blk[position][:, None] * h_now, axis=0))  36.7 us
    reduce_sum x32, other arithmetic, run_block(): decay = jnp.exp(a_trans * step_blk[position][None, :])  33.3 us
  transfers between devices with their start and end apart: 35, of which 35 were waited for; matrix products, arithmetic and copies ran while one was open for 0% of the time, Pallas kernels for 0%

profile of v1, /device:TPU:1, one launch (start us, length us, event | category | flops | bytes accessed | tf_op | source)
XLA Modules:
  0.0 852.6 jit_solution(17661322087214478475)
XLA Ops:
  14.2 38.7 %while.126 = (s32[]{:T(128)}, f32[16,2048]{1,0:T(8,128)S(1)}, f32[16,8,2048]{2,1,0:T(8,128)}, f32[16,2048]{1,0:T(8,128)S(1)}, f32[16,8,16]{2,1,0:T(8,128)}, /*in...) while((s32[]{:T(128)}, f32[16,2048]{1,0:T(8,128)S(1)}, ...), condition=%wide.region_2.3_spmd.clone, body=%wide.region_1.2_spmd.clone.sunk | while | flops 1097738 | bytes 985871 | solution.py:51
  54.0 95.3 %while.123 = (s32[]{:T(128)}, f32[1,16,2048]{2,1,0:T(8,128)S(1)}, f32[1,16,2048]{2,1,0:T(8,128)S(1)}, f32[1,16,2048]{2,1,0:T(8,128)S(1)}, s32[]{:T(128)}) while((s32[]{:T(128)}, f32[1,16,2048]{2,1,0:T(8,128)S(1)}, f32[1,16,2048]{2,1,0:T(8,128)S(1)}, f32[1,16,2048]{2,1,0:T(8,128)S(1)}, s32[]{:T(128)}) %tuple.427), condition=%wide.region_4.5_spmd, body=%wide.region_3.4_spmd.sunk | while | flops 65538 | bytes 1048677 | solution.py:153
  54.0 4.9 collective-permute-start
  59.0 1.9 collective-permute-done
  60.9 4.4 collective-permute-start
  65.3 1.9 collective-permute-done
  67.2 4.4 collective-permute-start
  71.6 1.9 collective-permute-done
  73.5 4.4 collective-permute-start
  77.9 1.9 collective-permute-done
  79.8 4.4 collective-permute-start
  84.2 1.9 collective-permute-done
  86.2 4.4 collective-permute-start
  90.5 1.9 collective-permute-done
  92.5 4.4 collective-permute-start
  96.8 1.9 collective-permute-done
  98.8 4.4 collective-permute-start
  103.1 1.9 collective-permute-done
  105.1 4.4 collective-permute-start
  109.5 1.9 collective-permute-done
  111.4 4.4 collective-permute-start
  115.8 1.9 collective-permute-done
  117.7 4.4 collective-permute-start
  122.1 1.9 collective-permute-done
  124.0 4.4 collective-permute-start
  128.4 1.9 collective-permute-done
  130.3 4.4 collective-permute-start
  134.7 1.9 collective-permute-done
  136.7 4.4 collective-permute-start
  141.0 1.9 collective-permute-done
  143.0 4.4 collective-permute-start
  147.3 1.9 collective-permute-done
  150.4 73.6 %while.124 = (s32[]{:T(128)}, f32[16,2048]{1,0:T(8,128)S(1)}, f32[16,16,2048]{2,1,0:T(8,128)}, f32[16,8,2048]{2,1,0:T(8,128)}, f32[16,8,2048]{2,1,0:T(8,128)}, /...) while((s32[]{:T(128)}, f32[16,2048]{1,0:T(8,128)S(1)}, ...), condition=%wide.region_14.15_spmd, body=%wide.region_5.0_spmd.sunk | while | flops 2359305 | bytes 2333341 | solution.py:51
  224.0 3.5 fusion.44
  227.5 43.2 %while.127 = (s32[]{:T(128)}, f32[16,2048]{1,0:T(8,128)S(1)}, f32[16,8,2048]{2,1,0:T(8,128)}, f32[16,2048]{1,0:T(8,128)S(1)}, f32[16,8,16]{2,1,0:T(8,128)}, /*in...) while((s32[]{:T(128)}, f32[16,2048]{1,0:T(8,128)S(1)}, ...), condition=%wide.region_16.17_spmd.clone, body=%wide.region_15.16_spmd.clone.sunk | while | flops 1081355 | bytes 789283 | solution.py:65
  243.9 1.9 constant_dynamic-slice_fusion.91
  270.7 114.7 %while.125 = (s32[]{:T(128)}, f32[1,16,2048]{2,1,0:T(8,128)S(1)}, f32[1,16,2048]{2,1,0:T(8,128)S(1)}, f32[1,16,2048]{2,1,0:T(8,128)S(1)}, s32[]{:T(128)}) while((s32[]{:T(128)}, f32[1,16,2048]{2,1,0:T(8,128)S(1)}, f32[1,16,2048]{2,1,0:T(8,128)S(1)}, f32[1,16,2048]{2,1,0:T(8,128)S(1)}, s32[]{:T(128)}) %tuple.426), condition=%wide.region_18.19_spmd, body=%wide.region_17.18_spmd.sunk | while | flops 65538 | bytes 1048677 | solution.py:154
  270.8 1.9 collective-permute-start.1
  272.7 5.7 collective-permute-done.1
  280.4 5.4 collective-permute-done.1
  287.8 6.3 collective-permute-done.1
  296.0 5.4 collective-permute-done.1
  303.4 6.3 collective-permute-done.1
  311.6 5.4 collective-permute-done.1
  319.0 6.3 collective-permute-done.1
  327.2 5.6 collective-permute-done.1
  334.8 5.6 collective-permute-done.1
  342.3 5.6 collective-permute-done.1
  349.8 5.6 collective-permute-done.1
  357.3 5.6 collective-permute-done.1
  364.9 5.6 collective-permute-done.1
  372.4 5.6 collective-permute-done.1
  379.9 5.6 collective-permute-done.1
  387.7 174.9 %while.128 = (s32[]{:T(128)}, f32[16,2048]{1,0:T(8,128)S(1)}, f32[16,2048]{1,0:T(8,128)S(1)}, f32[16,8,2048]{2,1,0:T(8,128)}, bf16[16,8,16]{2,1,0:T(8,128)(2,1)S...) while((s32[]{:T(128)}, f32[16,2048]{1,0:T(8,128)S(1)}, ...), condition=%wide.region_52.53_spmd.clone, body=%wide.region_19.52_spmd.clone.sunk | while | flops 8701451 | bytes 6086559 | solution.py:80
  453.5 1.9 constant_dynamic-slice_fusion.93
  567.6 3.3 collective-permute-done.2
  571.1 7.4 collective-permute-start.3
  578.5 33.2 %collective-permute-done.3 = f32[2048,180]{0,1:T(8,128)S(1)} collective-permute-done((f32[2048,180]{0,1:T(8,128)S(1)}, f32[2048,180]{0,1:T(8,128)S(1)}, u32[]{:S(2)}, u32[]{:S(2)}) %collective-permute-start.3) | collective-permute-done | bytes 1474592 | tf_op jit(solution)/shard_map/ppermute | solution.py:15
  611.9 14.4 %collective-permute-start.4 = (f32[2048,180]{0,1:T(8,128)S(1)}, f32[2048,180]{0,1:T(8,128)S(1)}, u32[]{:S(2)}, u32[]{:S(2)}) collective-permute-start(f32[2048,180]{0,1:T(8,128)S(1)} %add.420), channel_id=1, source_target_pairs={{0,4},{1,5},{2,6},{3,7},{4,0},{5,1},{6,2},{7,3},{8,12},{9,13},{10,... | collective-permute-start | bytes 4423688 | tf_op jit(solution)/shard_map/ppermute | solution.py:15
  626.3 65.0 %collective-permute-done.4 = f32[2048,180]{0,1:T(8,128)S(1)} collective-permute-done((f32[2048,180]{0,1:T(8,128)S(1)}, f32[2048,180]{0,1:T(8,128)S(1)}, u32[]{:S(2)}, u32[]{:S(2)}) %collective-permute-start.4) | collective-permute-done | bytes 1474592 | tf_op jit(solution)/shard_map/ppermute | solution.py:15
  691.6 3.2 collective-permute-start.5
  694.8 68.0 %collective-permute-done.5 = f32[2048,180]{0,1:T(8,128)S(1)} collective-permute-done((f32[2048,180]{0,1:T(8,128)S(1)}, f32[2048,180]{0,1:T(8,128)S(1)}, u32[]{:S(2)}, u32[]{:S(2)}) %collective-permute-start.5) | collective-permute-done | bytes 1474592 | tf_op jit(solution)/shard_map/ppermute | solution.py:15
  764.2 2.4 fusion.35
  766.6 72.5 %reduce-scatter.2.cloned.1.call-done = f32[128,180]{0,1:T(8,128)} async-done(((f32[2048,180]{0,1:T(8,128)}), f32[128,180]{0,1:T(8,128)}) %reduce-scatter.2.cloned.1.call-update) | async-done | bytes 92176 | tf_op jit(solution)/shard_map/reduce_scatter | solution.py:207
  (1178 shorter events, 372.0 us)
Async XLA Ops:
  7.2 1.4 copy-start
  7.2 4.8 copy-start.3
  7.2 4.8 copy-start.17
  7.2 5.0 copy-start.6
  7.2 5.0 copy-start.12
  7.2 831.9 %reduce-scatter.2.cloned.1.call-start = ((), (), s32[]{:S(2)}) async-start(), calls=%async_computation.1 | async-start | bytes 1601536 | tf_op jit(solution)/shard_map/reduce_scatter | solution.py:207
  9.9 4.3 copy-start.10
  12.2 550.5 %copy-start.15 = (f32[128]{0:T(128)}, f32[128]{0:T(128)S(1)}, u32[]{:S(2)}) copy-start(f32[128]{0:T(128)S(1)} %compare_convert_fusion) | copy-start | bytes 1540
  52.9 1.0 copy-start.2
  54.0 6.9 collective-permute-start
  60.9 6.3 collective-permute-start
  67.2 6.3 collective-permute-start
  73.5 6.3 collective-permute-start
  79.8 6.3 collective-permute-start
  86.2 6.3 collective-permute-start
  92.5 6.3 collective-permute-start
  98.8 6.3 collective-permute-start
  105.1 6.3 collective-permute-start
  111.4 6.3 collective-permute-start
  117.7 6.3 collective-permute-start
  124.0 6.3 collective-permute-start
  130.3 6.3 collective-permute-start
  136.7 6.3 collective-permute-start
  143.0 6.3 collective-permute-start
  150.4 73.6 %copy-start.1 = (bf16[1,128,2048]{2,1,0:T(8,128)(2,1)S(1)}, bf16[1,128,2048]{2,1,0:T(8,128)(2,1)}, u32[]{:S(2)}) copy-start(bf16[1,128,2048]{2,1,0:T(8,128)(2,1)} %param.23) | copy-start | bytes 1572868
  150.4 73.6 %copy-start.8 = (bf16[1,128,2048]{2,1,0:T(8,128)(2,1)S(1)}, bf16[1,128,2048]{2,1,0:T(8,128)(2,1)}, u32[]{:S(2)}) copy-start(bf16[1,128,2048]{2,1,0:T(8,128)(2,1)} %param.24) | copy-start | bytes 1572868
  150.4 73.6 %copy-start.13 = (f32[2048]{0:T(1024)S(1)}, f32[2048]{0:T(1024)}, u32[]{:S(2)}) copy-start(f32[2048]{0:T(1024)} %param.31) | copy-start | bytes 24580
  270.8 7.6 collective-permute-start.1
  278.4 7.4 collective-permute-start.1
  285.8 8.2 collective-permute-start.1
  294.1 7.4 collective-permute-start.1
  301.5 8.2 collective-permute-start.1
  309.7 7.4 collective-permute-start.1
  317.1 8.2 collective-permute-start.1
  325.3 7.5 collective-permute-start.1
  332.8 7.5 collective-permute-start.1
  340.4 7.5 collective-permute-start.1
  347.9 7.5 collective-permute-start.1
  355.4 7.5 collective-permute-start.1
  362.9 7.5 collective-permute-start.1
  370.5 7.5 collective-permute-start.1
  378.0 7.5 collective-permute-start.1
  562.7 1.7 copy-start.7
  562.7 2.0 copy-start.11
  562.7 3.1 copy-start.4
  567.5 3.4 collective-permute-start.2
  571.1 40.6 %collective-permute-start.3 = (f32[2048,180]{0,1:T(8,128)S(1)}, f32[2048,180]{0,1:T(8,128)S(1)}, u32[]{:S(2)}, u32[]{:S(2)}) collective-permute-start(f32[2048,180]{0,1:T(8,128)S(1)} %add.419), channel_id=1, source_target_pairs={{0,2},{1,3},{2,0},{3,1},{4,6},{5,7},{6,4},{7,5},{8,10},{9,11},{10,... | collective-permute-start | bytes 4423688 | tf_op jit(solution)/shard_map/ppermute | solution.py:15
  611.9 79.4 %collective-permute-start.4 = (f32[2048,180]{0,1:T(8,128)S(1)}, f32[2048,180]{0,1:T(8,128)S(1)}, u32[]{:S(2)}, u32[]{:S(2)}) collective-permute-start(f32[2048,180]{0,1:T(8,128)S(1)} %add.420), channel_id=1, source_target_pairs={{0,4},{1,5},{2,6},{3,7},{4,0},{5,1},{6,2},{7,3},{8,12},{9,13},{10,... | collective-permute-start | bytes 4423688 | tf_op jit(solution)/shard_map/ppermute | solution.py:15
  691.5 72.6 %copy-start.5 = (f32[16,8,2048]{2,1,0:T(8,128)S(1)}, f32[16,8,2048]{2,1,0:T(8,128)}, u32[]{:S(2)}) copy-start(f32[16,8,2048]{2,1,0:T(8,128)} %get-tuple-element.644) | copy-start | bytes 3145732
  691.5 72.6 %copy-start.9 = (bf16[1,128,2048]{2,1,0:T(8,128)(2,1)S(1)}, bf16[1,128,2048]{2,1,0:T(8,128)(2,1)}, u32[]{:S(2)}) copy-start(bf16[1,128,2048]{2,1,0:T(8,128)(2,1)} %param.24) | copy-start | bytes 1572868
  691.5 72.6 %copy-start.14 = (f32[2048]{0:T(1024)S(1)}, f32[2048]{0:T(1024)}, u32[]{:S(2)}) copy-start(f32[2048]{0:T(1024)} %param.31) | copy-start | bytes 24580
  691.6 72.6 %copy-start.16 = (f32[128]{0:T(128)S(1)}, f32[128]{0:T(128)}, u32[]{:S(2)}) copy-start(f32[128]{0:T(128)} %copy-done.15) | copy-start | bytes 1540
  691.6 71.2 %collective-permute-start.5 = (f32[2048,180]{0,1:T(8,128)S(1)}, f32[2048,180]{0,1:T(8,128)S(1)}, u32[]{:S(2)}, u32[]{:S(2)}) collective-permute-start(f32[2048,180]{0,1:T(8,128)S(1)} %add.421), channel_id=1, source_target_pairs={{0,8},{1,9},{2,10},{3,11},{4,12},{5,13},{6,14},{7,15},{8,0},{9,1},... | collective-permute-start | bytes 4423688 | tf_op jit(solution)/shard_map/ppermute | solution.py:15
Sparse Core Ops, SparseCore 0:
  764.3 74.7 reduce-scatter.1
